TPU v7x, 32 devices: a whole 2x2x4 slice. The times are simulated.
32 devices in a mesh: wide: 8 (over z, x), narrow: 4 (over y, core).
Axes of the slice: x: 2, y: 2, z: 4, core: 2. Of those that a mesh axis runs over, the one named last changes fastest.
Arguments:
- tokens: bfloat16 [26880, 768], P(('wide', 'narrow')), may hold values from -6 to 6
- patch_counts: int32 [96], P('wide'), may hold values from 100 to 240, as said below
- ln1_gain: float32 [768], replicated, may hold values from 0.25 to 1.75
- ln1_bias: float32 [768], replicated, may hold values from -3 to 3
- w_qkv: bfloat16 [768, 3, 768], P(None, None, 'narrow'), may hold values from -0.21875 to 0.21875
- b_qv: float32 [2, 768], P(None, 'narrow'), may hold values from -3 to 3
- w_out: bfloat16 [768, 768], P('narrow'), may hold values from -0.625 to 0.625
- b_out: float32 [768], replicated, may hold values from -3 to 3
- ln2_gain: float32 [768], replicated, may hold values from 0.25 to 1.75
- ln2_bias: float32 [768], replicated, may hold values from -3 to 3
- w_up: bfloat16 [768, 3072], P(None, 'narrow'), may hold values from -0.21875 to 0.21875
- b_up: bfloat16 [1, 3072], P(None, 'narrow'), may hold values from -3 to 3
- w_down: bfloat16 [3072, 768], P('narrow'), may hold values from -0.109375 to 0.109375
- b_down: float32 [768], replicated, may hold values from -3 to 3
- cotangent: bfloat16 [26880, 768], P(('wide', 'narrow')), may hold values from -6 to 6
Outputs:
- layer_out: float32 [26880, 768], P(('wide', 'narrow'))
- input_grad: float32 [26880, 768], P(('wide', 'narrow'))
- ln1_gain_grad: float32 [768], replicated
- ln1_bias_grad: float32 [768], replicated
- w_qkv_grad: float32 [768, 3, 768], P(None, None, 'narrow')
- b_qv_grad: float32 [2, 768], P(None, 'narrow')
- w_out_grad: float32 [768, 768], P('narrow')
- b_out_grad: float32 [768], replicated
- ln2_gain_grad: float32 [768], replicated
- ln2_bias_grad: float32 [768], replicated
- w_up_grad: float32 [768, 3072], P(None, 'narrow')
- b_up_grad: float32 [1, 3072], P(None, 'narrow')
- w_down_grad: float32 [3072, 768], P('narrow')
- b_down_grad: float32 [768], replicated
Inputs may be any that keep to these rules, and one draw needn't show every extreme that they name: patch_counts[i] is the number of real patches of item i; key positions 40 + patch_counts[i] and later of that item are padding.
All inputs are finite; a program needn't handle non-finite values.
Results may differ from a plain program's by a relative error of at most 0.012.
The roundings to bfloat16 on the way count: a program that leaves them out, or rounds other values in their place, can miss the bound.
Values may be sent and summed in bfloat16 or wider, within the bound.
No kernel may reach another device: no remote copies, remote signals or barrier semaphores. Data moves between devices by JAX's collectives and lax.ppermute only.
A program may use at most 192 MiB of HBM per device.

v0:
```python
import jax
import jax.numpy as jnp
from jax import lax
from jax.sharding import PartitionSpec as P

HEAD = 64
WORDS = 40
norm_eps = 1e-06
masked_value = -1000000000.0


def norm_parts(inputs, gain_row, bias_row):
    mean_rows = jnp.mean(inputs, axis=-1, keepdims=True)
    centred = inputs - mean_rows
    var_rows = jnp.mean(centred * centred, axis=-1, keepdims=True)
    inv_scale = lax.rsqrt(var_rows + norm_eps)
    unit_rows = centred * inv_scale
    return (unit_rows * gain_row + bias_row, unit_rows, inv_scale)


def norm_back(grad_rows, unit_rows, inv_scale, gain_row):
    scaled = grad_rows * gain_row
    inner = (
        scaled
        - jnp.mean(scaled, axis=-1, keepdims=True)
        - unit_rows * jnp.mean(scaled * unit_rows, axis=-1, keepdims=True)
    )
    return (inv_scale * inner, jnp.sum(grad_rows * unit_rows, axis=0), jnp.sum(grad_rows, axis=0))


def contract_rows(left_side, right_side):
    return lax.dot_general(
        left_side, right_side, (((0,), (0,)), ((), ())), preferred_element_type=jnp.float32
    )


def contract_cols(left_side, right_side):
    return lax.dot_general(
        left_side, right_side, (((1,), (1,)), ((), ())), preferred_element_type=jnp.float32
    )


def gelu_exact(inputs):
    return jax.nn.gelu(inputs, approximate=False)


def on_device(
    tokens,
    patch_counts,
    ln1_gain,
    ln1_bias,
    w_qkv,
    b_qv,
    w_out,
    b_out,
    ln2_gain,
    ln2_bias,
    w_up,
    b_up,
    w_down,
    b_down,
    cotangent,
):
    inputs = tokens.astype(jnp.float32)
    normed1, unit1, inv1 = norm_parts(inputs, ln1_gain, ln1_bias)
    normed1 = normed1.astype(jnp.bfloat16)
    grouped = lax.all_gather(normed1, "narrow", axis=0, tiled=True)
    full_out, full_down = (
        lax.all_gather(w_out, "narrow", axis=0, tiled=True),
        lax.all_gather(w_down, "narrow", axis=0, tiled=True),
    )
    full_up, full_up_bias = (
        lax.all_gather(w_up, "narrow", axis=1, tiled=True),
        lax.all_gather(b_up, "narrow", axis=1, tiled=True),
    )
    projected = jnp.einsum("td,dcf->tcf", grouped, w_qkv, preferred_element_type=jnp.float32)
    queries = ((projected[:, 0] + b_qv[0]) * 0.125).astype(jnp.bfloat16)
    key_rows = projected[:, 1].astype(jnp.bfloat16)
    value_rows = (projected[:, 2] + b_qv[1]).astype(jnp.bfloat16)
    item_count = patch_counts.shape[0]
    head_cols = w_qkv.shape[2]
    group_rows = grouped.shape[0]
    seq_len = group_rows // item_count
    shaped = (item_count, seq_len, head_cols // HEAD, HEAD)
    query_four = queries.reshape(shaped)
    key_four = key_rows.reshape(shaped)
    value_four = value_rows.reshape(shaped)
    positions = jnp.arange(seq_len)
    valid_keys = positions[None, :] < (WORDS + patch_counts)[:, None]
    key_mask = jnp.where(valid_keys, 0.0, masked_value).astype(jnp.float32)[:, None, None, :]
    scores = (
        jnp.einsum("iqhe,ikhe->ihqk", query_four, key_four, preferred_element_type=jnp.float32)
        + key_mask
    )
    row_max = jnp.max(scores, axis=-1, keepdims=True)
    shifted = jnp.exp(scores - row_max)
    row_total = jnp.sum(shifted, axis=-1, keepdims=True)
    log_total = row_max + jnp.log(row_total)
    weights = (shifted / row_total).astype(jnp.bfloat16)
    mixed = jnp.einsum("ihqk,ikhe->iqhe", weights, value_four, preferred_element_type=jnp.float32)
    mixed = mixed.astype(jnp.bfloat16).reshape(group_rows, head_cols)
    regrouped = lax.all_to_all(mixed, "narrow", split_axis=0, concat_axis=1, tiled=True)
    middle = inputs + (jnp.dot(regrouped, full_out, preferred_element_type=jnp.float32) + b_out)
    normed2, unit2, inv2 = norm_parts(middle, ln2_gain, ln2_bias)
    normed2 = normed2.astype(jnp.bfloat16)
    up_rows = jnp.dot(normed2, full_up, preferred_element_type=jnp.float32) + full_up_bias.astype(
        jnp.float32
    )
    activated, gelu_back = jax.vjp(gelu_exact, up_rows)
    hidden = activated.astype(jnp.bfloat16)
    layer_out = middle + jnp.dot(hidden, full_down, preferred_element_type=jnp.float32) + b_down
    grad_float = cotangent.astype(jnp.float32)
    grad_hidden = contract_cols(cotangent, full_down)
    grad_up = gelu_back(grad_hidden)[0].astype(jnp.bfloat16)
    grad_normed2 = contract_cols(grad_up, full_up)
    grad_norm_two, gain2_grad, bias2_grad = norm_back(grad_normed2, unit2, inv2, ln2_gain)
    grad_middle = grad_float + grad_norm_two
    grad_branch = grad_middle.astype(jnp.bfloat16)
    grad_mixed = contract_cols(grad_branch, full_out).astype(jnp.bfloat16)
    grad_heads = lax.all_to_all(grad_mixed, "narrow", split_axis=1, concat_axis=0, tiled=True)
    grad_four = grad_heads.reshape(shaped)
    scores_again = (
        jnp.einsum("iqhe,ikhe->ihqk", query_four, key_four, preferred_element_type=jnp.float32)
        + key_mask
    )
    prob_rows = jnp.exp(scores_again - log_total)
    weights_again = prob_rows.astype(jnp.bfloat16)
    grad_values = jnp.einsum(
        "ihqk,iqhe->ikhe", weights_again, grad_four, preferred_element_type=jnp.float32
    ).astype(jnp.bfloat16)
    grad_probs = jnp.einsum(
        "iqhe,ikhe->ihqk", grad_four, value_four, preferred_element_type=jnp.float32
    )
    grad_scores = (
        prob_rows * (grad_probs - jnp.sum(grad_probs * prob_rows, axis=-1, keepdims=True))
    ).astype(jnp.bfloat16)
    grad_queries = jnp.einsum(
        "ihqk,ikhe->iqhe", grad_scores, key_four, preferred_element_type=jnp.float32
    ).astype(jnp.bfloat16)
    grad_keys = jnp.einsum(
        "ihqk,iqhe->ikhe", grad_scores, query_four, preferred_element_type=jnp.float32
    ).astype(jnp.bfloat16)
    grad_queries = grad_queries.reshape(group_rows, head_cols) * 0.125
    grad_keys = grad_keys.reshape(group_rows, head_cols)
    grad_values = grad_values.reshape(group_rows, head_cols)
    grad_qkv = jnp.stack([grad_queries, grad_keys, grad_values], axis=1)
    w_qkv_grad = jnp.einsum("td,tcf->dcf", grouped, grad_qkv, preferred_element_type=jnp.float32)
    b_qv_grad = jnp.stack(
        [
            jnp.sum(grad_queries.astype(jnp.float32), axis=0),
            jnp.sum(grad_values.astype(jnp.float32), axis=0),
        ]
    )
    full_qkv = lax.all_gather(w_qkv, "narrow", axis=2, tiled=True)
    grad_qkv_own = lax.all_to_all(grad_qkv, "narrow", split_axis=0, concat_axis=2, tiled=True)
    grad_normed1 = jnp.einsum(
        "tcf,dcf->td", grad_qkv_own, full_qkv, preferred_element_type=jnp.float32
    )
    grad_norm_one, gain1_grad, bias1_grad = norm_back(grad_normed1, unit1, inv1, ln1_gain)
    input_grad = grad_middle + grad_norm_one
    out_bias_grad = jnp.sum(grad_branch.astype(jnp.float32), axis=0)
    down_bias_grad = jnp.sum(grad_float, axis=0)
    up_bias_full = jnp.sum(grad_up.astype(jnp.float32), axis=0, keepdims=True)
    out_whole = contract_rows(regrouped, grad_branch)
    down_whole = contract_rows(hidden, cotangent)
    out_part, down_part = (
        lax.psum_scatter(
            out_whole.astype(jnp.bfloat16), "narrow", scatter_dimension=0, tiled=True
        ).astype(jnp.float32),
        lax.psum_scatter(
            down_whole.astype(jnp.bfloat16), "narrow", scatter_dimension=0, tiled=True
        ).astype(jnp.float32),
    )
    up_whole = contract_rows(normed2, grad_up)
    up_part = lax.psum_scatter(
        up_whole.astype(jnp.bfloat16), "narrow", scatter_dimension=1, tiled=True
    ).astype(jnp.float32)
    summed = lax.psum((w_qkv_grad, b_qv_grad, out_part, up_part, down_part), "wide")
    small = lax.psum(
        (
            gain1_grad,
            bias1_grad,
            out_bias_grad,
            gain2_grad,
            bias2_grad,
            down_bias_grad,
            up_bias_full,
        ),
        ("wide", "narrow"),
    )
    shard_cols = b_up.shape[1]
    up_bias_grad = lax.dynamic_slice_in_dim(
        small[6], lax.axis_index("narrow") * shard_cols, shard_cols, 1
    )
    return (
        layer_out,
        input_grad,
        small[0],
        small[1],
        summed[0],
        summed[1],
        summed[2],
        small[2],
        small[3],
        small[4],
        summed[3],
        up_bias_grad,
        summed[4],
        small[5],
    )


def solution(mesh):
    placed = (
        P(("wide", "narrow"), None),
        P("wide"),
        P(),
        P(),
        P(None, None, "narrow"),
        P(None, "narrow"),
        P("narrow", None),
        P(),
        P(),
        P(),
        P(None, "narrow"),
        P(None, "narrow"),
        P("narrow", None),
        P(),
        P(("wide", "narrow"), None),
    )
    return jax.shard_map(
        on_device,
        mesh=mesh,
        in_specs=placed,
        out_specs=(
            P(("wide", "narrow"), None),
            P(("wide", "narrow"), None),
            P(),
            P(),
            P(None, None, "narrow"),
            P(None, "narrow"),
            P("narrow", None),
            P(),
            P(),
            P(),
            P(None, "narrow"),
            P(None, "narrow"),
            P("narrow", None),
            P(),
        ),
        check_vma=False,
    )
```

profile of v0, /device:TPU:0, one launch (start us, length us, event | category | flops | bytes accessed | tf_op | source)
XLA Modules:
  0.0 726.5 jit_solution(6485242681903960717)
XLA Ops:
  16.6 40.5 %all-gather.6.cloned.1.call-done = bf16[3360,768]{1,0:T(8,128)(2,1)} async-done(((bf16[840,768]{1,0:T(8,128)(2,1)}), bf16[3360,768]{1,0:T(8,128)(2,1)}) %all-gather.6.cloned.1.call-update) | async-done | bytes 5160976 | tf_op jit(solution)/shard_map/all_gather | solution.py:67
  57.1 5.5 fusion.47
  66.5 5.4 squeeze.8
  72.0 4.0 squeeze.7
  75.9 4.4 multiply_convert_fusion.2
  85.1 4.1 convert_element_type.106
  89.2 6.3 add_reduce_fusion
  101.7 5.6 convert_bitcast_fusion.2
  119.2 29.1 %all_gather.21 = bf16[1,3072]{1,0:T(2,128)(2,1)S(1)} all-gather(bf16[1,768]{1,0:T(2,128)(2,1)S(1)} %copy-done.34), channel_id=1, replica_groups=mesh['wide'=8,'narrow'=4] {'narrow'}, dimensions={1}, use_global_device_ids=true | all-gather | bytes 7680 | tf_op jit(solution)/shard_map/all_gather | solution.py:74
  153.6 11.5 %fusion.43 = f32[840,3072]{1,0:T(8,128)} fusion(bf16[768,3072]{1,0:T(8,128)(2,1)} %all-gather.10.cloned.1.call-done, f32[840,768]{1,0:T(8,128)} %copy-done.8, f32[768]{0:T(1024)S(1)} %copy-done.38, f32[768]{0:T(1024)S(1)} %copy-done.33, f32[840]{0:T(1024)S(1)} %add_rsqrt_fusion, f32[840]{0:T(1024)S(1)} %broadcast_multiply_fusion.4), kind=kOutput, calls=%fused_computation.104 | convolution fusion | flops 3966842880 | bytes 17633856 | tf_op jit(solution)/shard_map/dot_general | solution.py:106
  165.1 31.9 %convert_reduce_fusion = (f32[3072]{0:T(1024)S(1)}, bf16[840,3072]{1,0:T(8,128)(2,1)S(1)}, f32[840,3072]{1,0:T(8,128)}) fusion(f32[840,3072]{1,0:T(8,128)} %fusion.43, f32[3072]{0:T(1024)S(1)} %bitcast.79, bf16[840,768]{1,0:T(8,128)(2,1)S(1)} %copy-done.17, bf16[3072,768]{1,0:T(8,128)(2,1)} %all-gather.12.cloned.1.call-done), kind=kOutput, calls=%fused_computation.9 | convolution fusion | flops 4157150208 | bytes 31838208 | tf_op jit(solution)/shard_map/dot_general | solution.py:38
  197.0 4.7 multiply_reduce_fusion.1
  206.3 9.9 %convolution_convert_fusion.1 = bf16[768,3072]{1,0:T(8,128)(2,1)} fusion(bf16[840,3072]{1,0:T(8,128)(2,1)} %copy-done.42, f32[840,768]{1,0:T(8,128)} %copy-done.8, f32[768]{0:T(1024)S(1)} %copy-done.39, f32[768]{0:T(1024)S(1)} %copy-done.33, f32[840]{0:T(1024)S(1)} %add_rsqrt_fusion, f32[840]{0:T(1024)S(1)} %broadcast_multiply_fusion.4), kind=kOutput, calls=%fused_computation.31 | convolution fusion | flops 3969202176 | bytes 12472896 | tf_op jit(solution)/shard_map/dot_general | solution.py:32
  226.9 12.0 %multiply_convert_fusion.1 = bf16[840,3072]{1,0:T(8,128)(2,1)} fusion(f32[840,3072]{1,0:T(8,128)} %get-tuple-element.37, f32[840,3072]{1,0:T(8,128)} %fusion.43, f32[3072]{0:T(1024)S(1)} %bitcast.80), kind=kLoop, calls=%fused_computation.11 | loop fusion | flops 10321920 | bytes 25817088 | tf_op jit(solution)/shard_map/convert_element_type | solution.py:110
  238.9 10.3 %convolution_convert_fusion = bf16[3072,768]{1,0:T(8,128)(2,1)} fusion(bf16[840,3072]{1,0:T(8,128)(2,1)} %multiply_convert_fusion.1, bf16[840,768]{1,0:T(8,128)(2,1)S(1)} %copy-done.19), kind=kOutput, calls=%fused_computation.30 | convolution fusion | flops 3965976576 | bytes 11169792 | tf_op jit(solution)/shard_map/dot_general | solution.py:32
  251.4 3.9 reshape.150
  255.3 16.3 %multiply_reduce_fusion = (f32[12,3,280]{2,1,0:T(4,128)S(1)}, f32[12,3,280,280]{2,3,1,0:T(8,128)}) fusion(f32[12,3,280,280]{2,3,1,0:T(8,128)} %copy-done, f32[12,3,280]{2,1,0:T(4,128)S(1)} %log_add_fusion, f32[12,280]{1,0:T(8,128)S(1)} %copy-done.22, bf16[12,280,3,64]{1,0,3,2:T(8,128)(2,1)} %add_convert_fusion.1, bf16[12,280,3,64]{1,0,3,2:T(8,128)(2,1)S(1)} %reshape.150), kind=kOutput, calls=%fused_computation.2 | convolution fusion | flops 372546720 | bytes 25253760 | tf_op jit(solution)/shard_map/iqhe,ikhe->ihqk/dot_general | solution.py:131
  271.6 13.6 %multiply_convert_fusion = bf16[12,3,280,280]{2,3,1,0:T(8,128)(2,1)S(1)} fusion(f32[12,3,280,280]{2,3,1,0:T(8,128)} %get-tuple-element.49, f32[12,3,280,280]{2,3,1,0:T(8,128)} %copy-done, f32[12,3,280]{2,1,0:T(4,128)S(1)} %get-tuple-element.48, f32[12,3,280]{2,1,0:T(4,128)S(1)} %log_add_fusion, f32[12,280]{1,0:T(8,128)S(1)} %copy-done.22), kind=kLoop, calls=%fused_computation.1 | loop fusion | flops 14112000 | bytes 28318080 | tf_op jit(solution)/shard_map/convert_element_type | solution.py:136
  291.2 4.5 mul.189
  295.7 6.6 convert_bitcast_fusion.1
  304.9 4.3 stack_reshape.6
  309.2 7.3 %convert_reduce_fusion.2 = (f32[3,64]{1,0:T(4,128)S(1)}, bf16[12,280,3,64]{1,3,2,0:T(8,128)(2,1)S(1)}) fusion(f32[12,3,280,280]{2,3,1,0:T(8,128)} %copy-done, f32[12,3,280]{2,1,0:T(4,128)S(1)} %log_add_fusion, f32[12,280]{1,0:T(8,128)S(1)} %copy-done.22, bf16[12,280,3,64]{1,0,3,2:T(8,128)(2,1)S(1)} %reshape.150), kind=kOutput, calls=%fused_computation.37 | convolution fusion | flops 371669568 | bytes 13924608 | tf_op jit(solution)/shard_map/ihqk,iqhe->ikhe/dot_general | solution.py:128
  325.3 11.3 %copy.78 = bf16[3360,3,192]{2,1,0:T(4,128)(2,1)} copy(bf16[3360,3,192]{0,2,1:T(8,128)(2,1)} %constant_dynamic-update-slice_fusion) | data formatting | bytes 7741440 | tf_op jit(solution)/shard_map/stack | solution.py:146
  336.6 5.6 all-to-all-start.2
  342.5 9.5 %add_add_fusion = f32[840,768]{1,0:T(8,128)} fusion(f32[840,768]{1,0:T(8,128)S(1)} %copy-done.10, bf16[840,3072]{1,0:T(8,128)(2,1)} %multiply_convert_fusion.1, bf16[3072,768]{1,0:T(8,128)(2,1)} %all-gather.12.cloned.1.call-done, f32[768]{0:T(1024)S(1)} %copy-done.40), kind=kOutput, calls=%fused_computation.61 | convolution fusion | flops 3964907520 | bytes 15043584 | tf_op jit(solution)/shard_map/dot_general | solution.py:111
  352.2 8.2 %fusion.48 = f32[768,576]{0,1} fusion(bf16[3360,576]{0,1:T(8,128)(2,1)} %bitcast.15, bf16[3360,768]{1,0:T(8,128)(2,1)} %all-gather.6.cloned.1.call-done), kind=kOutput, calls=%fused_computation.108 | convolution fusion | flops 2972712960 | bytes 10801152
  360.5 78.4 %all-to-all-done.2 = bf16[3360,3,192]{2,1,0:T(4,128)(2,1)} async-done(((bf16[3360,3,192]{2,1,0:T(4,128)(2,1)}), bf16[3360,3,192]{2,1,0:T(4,128)(2,1)}, u32[]{:S(2)}, u32[]{:S(2)}) %all-to-all-start.2) | async-done | bytes 3870752 | tf_op jit(solution)/shard_map/all_to_all | solution.py:155
  439.0 11.4 %copy.79 = bf16[4,840,3,192]{1,3,0,2:T(8,128)(2,1)} copy(bf16[4,840,3,192]{3,2,1,0:T(4,128)(2,1)} %bitcast.11) | data formatting | bytes 7741440 | tf_op jit(solution)/shard_map/all_to_all | solution.py:155
  450.4 8.6 %fusion.25 = (f32[768]{0:T(1024)S(1)}, f32[840]{0:T(1024)S(1)}, f32[840]{0:T(1024)S(1)}, f32[768]{0:T(1024)S(1)}, f32[840,768,1]{1,0,2:T(8,128)}) fusion(bf16[840,768]{1,0:T(8,128)(2,1)S(1)} %copy-done.3, f32[840]{0:T(1024)S(1)} %copy-done.31, f32[840]{0:T(1024)S(1)} %copy-done.29, f32[768]{0:T(1024)S(1)} %copy-done.32, bf16[840,3,768]{0,2,1:T(8,128)(2,1)} %bitcast.74, ...), kind=kOutput, calls=%fused_computation.54 | convolution fusion | flops 2979161088 | bytes 11303040 | tf_op jit(solution)/shard_map/tcf,dcf->td/dot_general | solution.py:156
  458.9 41.5 %all-reduce = (f32[768]{0:T(1024)}, f32[768]{0:T(1024)}, f32[768]{0:T(1024)}, f32[768]{0:T(1024)}, f32[768]{0:T(1024)}, /*index=5*/f32[1,3072]{1,0:T(1,128)S(1)}, f32[768]{0:T(1024)}) all-reduce(f32[768]{0:T(1024)S(1)} %get-tuple-element.16, f32[768]{0:T(1024)S(1)} %get-tuple-element.21, ...), channel_id=1, replica_groups=mesh['wide'=8,'narrow'=4] {'wide','narrow'}, use_global_device_ids=true, to_apply=%region_12.13 | all-reduce | flops 7680 | bytes 61440 | tf_op jit(solution)/shard_map/psum | solution.py:179
  501.0 4.1 fusion.24
  505.1 211.7 %all-reduce.6 = (f32[2,192]{1,0:T(2,128)}, f32[192,768]{1,0:T(8,128)}, f32[768,768]{1,0:T(8,128)}, f32[768,768]{1,0:T(8,128)}) all-reduce(f32[2,192]{1,0:T(2,128)S(1)} %pad_maximum_fusion, bf16[192,768]{1,0:T(8,128)(2,1)S(1)} %copy-done.27, ...), channel_id=1, replica_groups=mesh['wide'=8,'narrow'=4] {'wide'}, use_global_device_ids=true, to_apply=%region_18.19 | all-reduce | flops 1327488 | bytes 7965696 | tf_op jit(solution)/shard_map/psum | solution.py:178
  (160 shorter events, 79.6 us)
Async XLA Ops:
  7.2 49.9 %all-gather.6.cloned.1.call-start = ((), (), s32[]{:S(2)}) async-start(), calls=%async_computation.6 | async-start | bytes 6451200 | tf_op jit(solution)/shard_map/all_gather | solution.py:67
  10.7 46.4 %copy-start.20 = (bf16[768,3,192]{0,2,1:T(8,128)(2,1)S(1)}, bf16[768,3,192]{0,2,1:T(8,128)(2,1)}, u32[]{:S(2)}) copy-start(bf16[768,3,192]{0,2,1:T(8,128)(2,1)} %param.19) | copy-start | bytes 2654212
  14.2 134.1 %all-gather.8.cloned.1.call-start = ((), (), s32[]{:S(2)}) async-start(), calls=%async_computation.7 | async-start | bytes 1474560 | tf_op jit(solution)/shard_map/all_gather | solution.py:69
  15.0 138.6 %all-gather.10.cloned.1.call-start = ((), (), s32[]{:S(2)}) async-start(), calls=%async_computation.8 | async-start | bytes 5898240 | tf_op jit(solution)/shard_map/all_gather | solution.py:73
  15.7 149.4 %all-gather.12.cloned.1.call-start = ((), (), s32[]{:S(2)}) async-start(), calls=%async_computation.9 | async-start | bytes 5898240 | tf_op jit(solution)/shard_map/all_gather | solution.py:70
  16.4 82.5 %copy-start.21 = (f32[12,280]{1,0:T(8,128)}, f32[12,280]{1,0:T(8,128)S(1)}, u32[]{:S(2)}) copy-start(f32[12,280]{1,0:T(8,128)S(1)} %fusion.40) | copy-start | bytes 40324
  89.2 6.4 copy-start.4
  95.6 6.1 copy-start
  95.6 6.1 copy-start.23
  95.6 6.1 copy-start.11
  112.9 6.3 copy-start.34
  112.9 35.5 %copy-start.2 = (bf16[840,768]{1,0:T(8,128)(2,1)S(1)}, bf16[840,768]{1,0:T(8,128)(2,1)}, u32[]{:S(2)}) copy-start(bf16[840,768]{1,0:T(8,128)(2,1)} %param.15) | copy-start | bytes 3870724
  112.9 35.5 %copy-start.37 = (f32[768]{0:T(1024)S(1)}, f32[768]{0:T(1024)}, u32[]{:S(2)}) copy-start(f32[768]{0:T(1024)} %param.22) | copy-start | bytes 9220
  115.6 32.8 %all-to-all-start = ((bf16[4,840,192]{1,2,0:T(8,128)(2,1)}), bf16[4,840,192]{1,2,0:T(8,128)(2,1)S(1)}, u32[]{:S(2)}, u32[]{:S(2)}) async-start(bf16[4,840,192]{1,2,0:T(8,128)(2,1)} %copy.64), calls=%async_computation | async-start | bytes 2752512 | tf_op jit(solution)/shard_map/all_to_all | solution.py:102
  119.1 241.4 %reduce-scatter.4.cloned.1.call-start = ((), (), s32[]{:S(2)}) async-start(), calls=%async_computation.12 | async-start | bytes 1474560 | tf_op jit(solution)/shard_map/reduce_scatter | solution.py:167
  153.6 11.5 %copy-start.17 = (bf16[840,768]{1,0:T(8,128)(2,1)S(1)}, bf16[840,768]{1,0:T(8,128)(2,1)}, u32[]{:S(2)}) copy-start(bf16[840,768]{1,0:T(8,128)(2,1)} %param.29) | copy-start | bytes 3870724
  165.1 31.9 %copy-start.9 = (f32[840,768]{1,0:T(8,128)S(1)}, f32[840,768]{1,0:T(8,128)}, u32[]{:S(2)}) copy-start(f32[840,768]{1,0:T(8,128)} %copy-done.8) | copy-start | bytes 7741444
  165.1 31.9 %copy-start.36 = (bf16[768,3072]{1,0:T(8,128)(2,1)S(1)}, bf16[768,3072]{1,0:T(8,128)(2,1)}, u32[]{:S(2)}) copy-start(bf16[768,3072]{1,0:T(8,128)(2,1)} %all-gather.10.cloned.1.call-done) | copy-start | bytes 14155780
  203.2 14.0 %copy-start.7 = (f32[840,768]{1,0:T(8,128)}, f32[840,768]{1,0:T(8,128)S(1)}, u32[]{:S(2)}) copy-start(f32[840,768]{1,0:T(8,128)S(1)} %get-tuple-element.39) | copy-start | bytes 7741444
  205.7 244.7 %all-gather.14.cloned.1.call-start = ((), (), s32[]{:S(2)}) async-start(), calls=%async_computation.10 | async-start | bytes 4423680 | tf_op jit(solution)/shard_map/all_gather | solution.py:154
  206.2 298.8 %reduce-scatter.6.cloned.1.call-start = ((), (), s32[]{:S(2)}) async-start(), calls=%async_computation.13 | async-start | bytes 5898240 | tf_op jit(solution)/shard_map/reduce_scatter | solution.py:175
  223.3 26.0 %all-to-all-start.1 = ((bf16[840,4,192]{0,2,1:T(8,128)(2,1)}), bf16[840,4,192]{0,2,1:T(8,128)(2,1)S(1)}, u32[]{:S(2)}, u32[]{:S(2)}) async-start(bf16[840,4,192]{0,2,1:T(8,128)(2,1)} %bitcast.6), calls=%async_computation.1 | async-start | bytes 2752512 | tf_op jit(solution)/shard_map/all_to_all | solution.py:120
  226.8 278.2 %reduce-scatter.8.cloned.1.call-start = ((), (), s32[]{:S(2)}) async-start(), calls=%async_computation.14 | async-start | bytes 5898240 | tf_op jit(solution)/shard_map/reduce_scatter | solution.py:170
  226.9 12.0 %copy-start.19 = (bf16[840,768]{1,0:T(8,128)(2,1)S(1)}, bf16[840,768]{1,0:T(8,128)(2,1)}, u32[]{:S(2)}) copy-start(bf16[840,768]{1,0:T(8,128)(2,1)} %param.29) | copy-start | bytes 3870724
  249.2 6.1 copy-start.22
  271.6 13.7 %copy-start.5 = (bf16[12,280,3,64]{1,0,3,2:T(8,128)(2,1)S(1)}, bf16[12,280,3,64]{1,0,3,2:T(8,128)(2,1)}, u32[]{:S(2)}) copy-start(bf16[12,280,3,64]{1,0,3,2:T(8,128)(2,1)} %copy-done.4) | copy-start | bytes 3870724
  336.6 102.4 %all-to-all-start.2 = ((bf16[3360,3,192]{2,1,0:T(4,128)(2,1)}), bf16[3360,3,192]{2,1,0:T(4,128)(2,1)}, u32[]{:S(2)}, u32[]{:S(2)}) async-start(bf16[3360,3,192]{2,1,0:T(4,128)(2,1)} %copy.78), calls=%async_computation.2 | async-start | bytes 13762560 | tf_op jit(solution)/shard_map/all_to_all | solution.py:155
  342.2 374.5 %all-reduce.5.cloned.1.call-start = ((), (), s32[]{:S(2)}) async-start(), calls=%async_computation.11 | async-start | bytes 3538944 | tf_op jit(solution)/shard_map/psum | solution.py:178
  439.0 11.4 %copy-start.3 = (bf16[840,768]{1,0:T(8,128)(2,1)S(1)}, bf16[840,768]{1,0:T(8,128)(2,1)}, u32[]{:S(2)}) copy-start(bf16[840,768]{1,0:T(8,128)(2,1)} %param.15) | copy-start | bytes 3870724
  439.0 11.4 %copy-start.29 = (f32[840]{0:T(1024)S(1)}, f32[840]{0:T(1024)}, u32[]{:S(2)}) copy-start(f32[840]{0:T(1024)} %copy-done.28) | copy-start | bytes 10084
  439.0 11.4 %copy-start.31 = (f32[840]{0:T(1024)S(1)}, f32[840]{0:T(1024)}, u32[]{:S(2)}) copy-start(f32[840]{0:T(1024)} %copy-done.30) | copy-start | bytes 10084
  439.0 11.4 %copy-start.32 = (f32[768]{0:T(1024)S(1)}, f32[768]{0:T(1024)}, u32[]{:S(2)}) copy-start(f32[768]{0:T(1024)} %param.17) | copy-start | bytes 9220
  (23 other events, 84.7 us)
Sparse Core Ops, SparseCore 0:
  14.3 42.6 all-gather.5
  58.6 17.4 all-gather.7
  77.7 37.4 all-gather.9
  116.6 47.4 all-gather.11
  205.8 25.8 reduce-scatter.3
  233.2 32.4 all-gather.13
  268.3 47.8 reduce-scatter.5
  318.7 67.6 reduce-scatter.7
  391.0 94.6 all-reduce.4
where the time goes:
time: 738 us; the launch traced here: 727 us
  blocking collectives  282 us (38%)
  matrix products  154 us (21%)
  waiting for transfers between devices  121 us (16%)
  local copies, waits for them, and re-layouts  93.5 us (13%)
  other arithmetic  47.4 us (6%)
  between operations  14.9 us (2%)
  starting transfers between devices  13.3 us (2%)
    psum x1, blocking collectives, on_device(): lax.psum((w_qkv_grad, b_qv_grad, out_part, up_part, down_part), 'wide')  212 us
    all_to_all x1, waiting for transfers between devices, on_device(): lax.all_to_all(grad_qkv, 'narrow', split_axis=0, concat_axis=2, tiled=True)  78.4 us
    psum x1, blocking collectives, on_device(): lax.psum((gain1_grad, bias1_grad, out_bias_grad, gain2_grad, bias2_grad,...  41.5 us
    all_gather x1, waiting for transfers between devices, on_device(): grouped = lax.all_gather(normed1, 'narrow', axis=0, tiled=True)  40.5 us
    dot_general x3, matrix products, contract_cols(): lax.dot_general(left_side, right_side, (((1,), (1,)), ((), ())), preferre...  40.2 us
    all_gather x1, blocking collectives, on_device(): lax.all_gather(b_up, 'narrow', axis=1, tiled=True)  29.1 us
    dot_general x3, matrix products, contract_rows(): lax.dot_general(left_side, right_side, (((0,), (0,)), ((), ())), preferre...  22.7 us
    another operation x4, local copies, waits for them, and re-layouts, on_device(): grad_qkv = jnp.stack([grad_queries, grad_keys, grad_values], axis=1)  19.5 us
  transfers between devices with their start and end apart: 12, of which 2 were waited for; matrix products, arithmetic and copies ran while one was open for 32% of the time, Pallas kernels for 0%

commit v1 on v0

--- a/solution.py
+++ b/solution.py
@@ -7,6 +7,16 @@
 WORDS = 40
 norm_eps = 1e-06
 masked_value = -1000000000.0
+
+
+def use_forms(buf):
+    row_out = lax.axis_size("narrow")
+    res = jnp.split(buf, row_out, axis=0)
+    state_next = jnp.stack(res)
+    current_arr = jnp.concatenate(
+        lax.all_to_all(state_next, axis_name="narrow", split_axis=0, concat_axis=0), axis=2
+    )
+    return current_arr
 
 
 def norm_parts(inputs, gain_row, bias_row):
@@ -152,7 +162,7 @@
         ]
     )
     full_qkv = lax.all_gather(w_qkv, "narrow", axis=2, tiled=True)
-    grad_qkv_own = lax.all_to_all(grad_qkv, "narrow", split_axis=0, concat_axis=2, tiled=True)
+    grad_qkv_own = use_forms(grad_qkv)
     grad_normed1 = jnp.einsum(
         "tcf,dcf->td", grad_qkv_own, full_qkv, preferred_element_type=jnp.float32
     )

time: 738 us -> 705 us (0.955)
  waiting for transfers between devices: 121 us -> 97.4 us
  local copies, waits for them, and re-layouts: 93.5 us -> 77 us
    all_to_all x1, waiting for transfers between devices: 78.4 us -> 54.4 us  [use_forms(): lax.all_to_all(state_next, axis_name='narrow', split_axis=0, concat_axis=0)]
    another operation x4 -> x3, local copies, waits for them, and re-layouts: 19.5 us -> 7.24 us  [on_device(): grad_qkv = jnp.stack([grad_queries, grad_keys, grad_values], axis=1)]
    all_to_all x1 -> x0, local copies, waits for them, and re-layouts: 11.4 us -> none  [on_device(): lax.all_to_all(grad_qkv, 'narrow', split_axis=0, concat_axis=2, tiled=True)]
  transfers between devices with their start and end apart: 12 -> 12, of which waited for: 2 -> 2; matrix products, arithmetic and copies ran while one was open for 32% -> 31% of each run, Pallas kernels for 0% -> 0%
where the time goes in v1:
time: 705 us; the launch traced here: 694 us
  blocking collectives  287 us (41%)
  matrix products  154 us (22%)
  waiting for transfers between devices  97.4 us (14%)
  local copies, waits for them, and re-layouts  77 us (11%)
  other arithmetic  50.1 us (7%)
  between operations  14.9 us (2%)
  starting transfers between devices  13 us (2%)
    psum x1, blocking collectives, on_device(): lax.psum((w_qkv_grad, b_qv_grad, out_part, up_part, down_part), 'wide')  216 us
    all_to_all x1, waiting for transfers between devices, use_forms(): lax.all_to_all(state_next, axis_name='narrow', split_axis=0, concat_axis=0)  54.4 us
    psum x1, blocking collectives, on_device(): lax.psum((gain1_grad, bias1_grad, out_bias_grad, gain2_grad, bias2_grad,...  40.7 us
    all_gather x1, waiting for transfers between devices, on_device(): grouped = lax.all_gather(normed1, 'narrow', axis=0, tiled=True)  40.5 us
    dot_general x3, matrix products, contract_cols(): lax.dot_general(left_side, right_side, (((1,), (1,)), ((), ())), preferre...  40.2 us
    all_gather x1, blocking collectives, on_device(): lax.all_gather(b_up, 'narrow', axis=1, tiled=True)  30.5 us
    dot_general x3, matrix products, contract_rows(): lax.dot_general(left_side, right_side, (((0,), (0,)), ((), ())), preferre...  23.2 us
    dot_general x1, matrix products, on_device(): jnp.einsum('iqhe,ikhe->ihqk', grad_four, value_four, preferred_element_ty...  16.4 us
  transfers between devices with their start and end apart: 12, of which 2 were waited for; matrix products, arithmetic and copies ran while one was open for 31% of the time, Pallas kernels for 0%

profile of v1, /device:TPU:0, one launch (start us, length us, event | category | flops | bytes accessed | tf_op | source)
XLA Modules:
  0.0 694.0 jit_solution(14273363866613842925)
XLA Ops:
  16.6 40.5 %all-gather.6.cloned.1.call-done = bf16[3360,768]{1,0:T(8,128)(2,1)} async-done(((bf16[840,768]{1,0:T(8,128)(2,1)}), bf16[3360,768]{1,0:T(8,128)(2,1)}) %all-gather.6.cloned.1.call-update) | async-done | bytes 5160976 | tf_op jit(solution)/shard_map/all_gather | solution.py:77
  57.1 5.5 fusion.47
  66.6 5.4 squeeze.8
  72.0 4.0 squeeze.7
  76.0 4.4 multiply_convert_fusion.2
  85.2 4.1 convert_element_type.106
  89.3 6.3 add_reduce_fusion
  101.8 5.6 convert_bitcast_fusion.2
  107.4 4.0 copy.63
  111.4 4.2 all_to_all.29
  120.7 30.5 %all_gather.21 = bf16[1,3072]{1,0:T(2,128)(2,1)S(1)} all-gather(bf16[1,768]{1,0:T(2,128)(2,1)S(1)} %copy-done.34), channel_id=1, replica_groups=mesh['wide'=8,'narrow'=4] {'narrow'}, dimensions={1}, use_global_device_ids=true | all-gather | bytes 7680 | tf_op jit(solution)/shard_map/all_gather | solution.py:84
  156.6 11.5 %fusion.43 = f32[840,3072]{1,0:T(8,128)} fusion(bf16[768,3072]{1,0:T(8,128)(2,1)} %all-gather.10.cloned.1.call-done, f32[840,768]{1,0:T(8,128)} %copy-done.8, f32[768]{0:T(1024)S(1)} %copy-done.38, f32[768]{0:T(1024)S(1)} %copy-done.33, f32[840]{0:T(1024)S(1)} %add_rsqrt_fusion, f32[840]{0:T(1024)S(1)} %broadcast_multiply_fusion.4), kind=kOutput, calls=%fused_computation.109 | convolution fusion | flops 3966842880 | bytes 17633856 | tf_op jit(solution)/shard_map/dot_general | solution.py:116
  168.1 31.8 %convert_reduce_fusion = (f32[3072]{0:T(1024)S(1)}, bf16[840,3072]{1,0:T(8,128)(2,1)S(1)}, f32[840,3072]{1,0:T(8,128)}) fusion(f32[840,3072]{1,0:T(8,128)} %fusion.43, f32[3072]{0:T(1024)S(1)} %bitcast.86, bf16[840,768]{1,0:T(8,128)(2,1)S(1)} %copy-done.17, bf16[3072,768]{1,0:T(8,128)(2,1)} %all-gather.12.cloned.1.call-done), kind=kOutput, calls=%fused_computation.9 | convolution fusion | flops 4157150208 | bytes 31838208 | tf_op jit(solution)/shard_map/dot_general | solution.py:48
  200.0 4.7 multiply_reduce_fusion.1
  209.3 10.3 %convolution_convert_fusion.1 = bf16[768,3072]{1,0:T(8,128)(2,1)} fusion(bf16[840,3072]{1,0:T(8,128)(2,1)} %copy-done.42, f32[840,768]{1,0:T(8,128)} %copy-done.8, f32[768]{0:T(1024)S(1)} %copy-done.39, f32[768]{0:T(1024)S(1)} %copy-done.33, f32[840]{0:T(1024)S(1)} %add_rsqrt_fusion, f32[840]{0:T(1024)S(1)} %broadcast_multiply_fusion.4), kind=kOutput, calls=%fused_computation.31 | convolution fusion | flops 3969202176 | bytes 12472896 | tf_op jit(solution)/shard_map/dot_general | solution.py:42
  230.4 12.0 %multiply_convert_fusion.1 = bf16[840,3072]{1,0:T(8,128)(2,1)} fusion(f32[840,3072]{1,0:T(8,128)} %get-tuple-element.37, f32[840,3072]{1,0:T(8,128)} %fusion.43, f32[3072]{0:T(1024)S(1)} %bitcast.87), kind=kLoop, calls=%fused_computation.11 | loop fusion | flops 10321920 | bytes 25817088 | tf_op jit(solution)/shard_map/convert_element_type | solution.py:120
  242.4 10.4 %convolution_convert_fusion = bf16[3072,768]{1,0:T(8,128)(2,1)} fusion(bf16[840,3072]{1,0:T(8,128)(2,1)} %multiply_convert_fusion.1, bf16[840,768]{1,0:T(8,128)(2,1)S(1)} %copy-done.19), kind=kOutput, calls=%fused_computation.30 | convolution fusion | flops 3965976576 | bytes 11169792 | tf_op jit(solution)/shard_map/dot_general | solution.py:42
  258.8 16.4 %multiply_reduce_fusion = (f32[12,3,280]{2,1,0:T(4,128)S(1)}, f32[12,3,280,280]{2,3,1,0:T(8,128)}) fusion(f32[12,3,280,280]{2,3,1,0:T(8,128)} %copy-done, f32[12,3,280]{2,1,0:T(4,128)S(1)} %log_add_fusion, f32[12,280]{1,0:T(8,128)S(1)} %copy-done.22, bf16[12,280,3,64]{1,0,3,2:T(8,128)(2,1)} %add_convert_fusion.1, bf16[12,280,3,64]{1,0,3,2:T(8,128)(2,1)S(1)} %reshape.156), kind=kOutput, calls=%fused_computation.2 | convolution fusion | flops 372546720 | bytes 25253760 | tf_op jit(solution)/shard_map/iqhe,ikhe->ihqk/dot_general | solution.py:141
  275.2 13.7 %multiply_convert_fusion = bf16[12,3,280,280]{2,3,1,0:T(8,128)(2,1)S(1)} fusion(f32[12,3,280,280]{2,3,1,0:T(8,128)} %get-tuple-element.53, f32[12,3,280,280]{2,3,1,0:T(8,128)} %copy-done, f32[12,3,280]{2,1,0:T(4,128)S(1)} %get-tuple-element.52, f32[12,3,280]{2,1,0:T(4,128)S(1)} %log_add_fusion, f32[12,280]{1,0:T(8,128)S(1)} %copy-done.22), kind=kLoop, calls=%fused_computation.1 | loop fusion | flops 14112000 | bytes 28318080 | tf_op jit(solution)/shard_map/convert_element_type | solution.py:146
  294.8 4.5 mul.189
  299.3 6.6 convert_bitcast_fusion.1
  308.5 4.3 stack_reshape.6
  312.8 7.2 %convert_reduce_fusion.2 = (f32[3,64]{1,0:T(4,128)S(1)}, bf16[12,280,3,64]{1,3,2,0:T(8,128)(2,1)S(1)}) fusion(f32[12,3,280,280]{2,3,1,0:T(8,128)} %copy-done, f32[12,3,280]{2,1,0:T(4,128)S(1)} %log_add_fusion, f32[12,280]{1,0:T(8,128)S(1)} %copy-done.22, bf16[12,280,3,64]{1,0,3,2:T(8,128)(2,1)S(1)} %reshape.156), kind=kOutput, calls=%fused_computation.38 | convolution fusion | flops 371669568 | bytes 13924608 | tf_op jit(solution)/shard_map/ihqk,iqhe->ikhe/dot_general | solution.py:138
  331.7 5.1 all-to-all-start.2
  337.1 9.6 %add_add_fusion = f32[840,768]{1,0:T(8,128)} fusion(f32[840,768]{1,0:T(8,128)S(1)} %copy-done.10, bf16[840,3072]{1,0:T(8,128)(2,1)} %multiply_convert_fusion.1, bf16[3072,768]{1,0:T(8,128)(2,1)} %all-gather.12.cloned.1.call-done, f32[768]{0:T(1024)S(1)} %copy-done.40), kind=kOutput, calls=%fused_computation.62 | convolution fusion | flops 3964907520 | bytes 15043584 | tf_op jit(solution)/shard_map/dot_general | solution.py:121
  346.9 8.2 %fusion.48 = f32[768,576]{0,1} fusion(bf16[3360,576]{0,1:T(8,128)(2,1)} %bitcast.77, bf16[3360,768]{1,0:T(8,128)(2,1)} %all-gather.6.cloned.1.call-done), kind=kOutput, calls=%fused_computation.113 | convolution fusion | flops 2972712960 | bytes 10801152
  355.2 54.4 %all-to-all-done.2 = bf16[4,840,3,192]{1,3,2,0:T(8,128)(2,1)} async-done(((bf16[4,840,3,192]{1,3,2,0:T(8,128)(2,1)}), bf16[4,840,3,192]{1,3,2,0:T(8,128)(2,1)}, u32[]{:S(2)}, u32[]{:S(2)}) %all-to-all-start.2) | async-done | bytes 3870752 | tf_op jit(solution)/shard_map/all_to_all | solution.py:17
  409.6 4.6 copy.78
  414.2 8.6 %fusion.25 = (f32[768]{0:T(1024)S(1)}, f32[840]{0:T(1024)S(1)}, f32[840]{0:T(1024)S(1)}, f32[768]{0:T(1024)S(1)}, f32[840,768,1]{1,0,2:T(8,128)}) fusion(bf16[840,768]{1,0:T(8,128)(2,1)S(1)} %copy-done.3, f32[840]{0:T(1024)S(1)} %copy-done.31, f32[840]{0:T(1024)S(1)} %copy-done.29, f32[768]{0:T(1024)S(1)} %copy-done.32, bf16[840,3,768]{0,2,1:T(8,128)(2,1)} %bitcast.81, ...), kind=kOutput, calls=%fused_computation.55 | convolution fusion | flops 2979161088 | bytes 11303040 | tf_op jit(solution)/shard_map/tcf,dcf->td/dot_general | solution.py:166
  422.8 40.7 %all-reduce = (f32[768]{0:T(1024)}, f32[768]{0:T(1024)}, f32[768]{0:T(1024)}, f32[768]{0:T(1024)}, f32[768]{0:T(1024)}, /*index=5*/f32[1,3072]{1,0:T(1,128)S(1)}, f32[768]{0:T(1024)}) all-reduce(f32[768]{0:T(1024)S(1)} %get-tuple-element.16, f32[768]{0:T(1024)S(1)} %get-tuple-element.21, ...), channel_id=1, replica_groups=mesh['wide'=8,'narrow'=4] {'wide','narrow'}, use_global_device_ids=true, to_apply=%region_12.13 | all-reduce | flops 7680 | bytes 61440 | tf_op jit(solution)/shard_map/psum | solution.py:189
  464.0 4.1 fusion.24
  468.1 216.1 %all-reduce.6 = (f32[2,192]{1,0:T(2,128)}, f32[192,768]{1,0:T(8,128)}, f32[768,768]{1,0:T(8,128)}, f32[768,768]{1,0:T(8,128)}) all-reduce(f32[2,192]{1,0:T(2,128)S(1)} %pad_maximum_fusion.1, bf16[192,768]{1,0:T(8,128)(2,1)S(1)} %copy-done.27, ...), channel_id=1, replica_groups=mesh['wide'=8,'narrow'=4] {'wide'}, use_global_device_ids=true, to_apply=%region_18.19 | all-reduce | flops 1327488 | bytes 7965696 | tf_op jit(solution)/shard_map/psum | solution.py:188
  (161 shorter events, 79.7 us)
Async XLA Ops:
  7.2 49.9 %all-gather.6.cloned.1.call-start = ((), (), s32[]{:S(2)}) async-start(), calls=%async_computation.6 | async-start | bytes 6451200 | tf_op jit(solution)/shard_map/all_gather | solution.py:77
  8.8 7.6 %copy-start.41 = (s32[12]{0:T(128)S(1)}, s32[12]{0:T(128)}, u32[]{:S(2)}) copy-start(s32[12]{0:T(128)} %param.16) | copy-start | bytes 148
  8.8 7.7 %copy-start.35 = (f32[2,192]{1,0:T(2,128)S(1)}, f32[2,192]{1,0:T(2,128)}, u32[]{:S(2)}) copy-start(f32[2,192]{1,0:T(2,128)} %param.20) | copy-start | bytes 4612
  8.8 48.3 %copy-start.20 = (bf16[768,3,192]{0,2,1:T(8,128)(2,1)S(1)}, bf16[768,3,192]{0,2,1:T(8,128)(2,1)}, u32[]{:S(2)}) copy-start(bf16[768,3,192]{0,2,1:T(8,128)(2,1)} %param.19) | copy-start | bytes 2654212
  14.3 137.0 %all-gather.8.cloned.1.call-start = ((), (), s32[]{:S(2)}) async-start(), calls=%async_computation.7 | async-start | bytes 1474560 | tf_op jit(solution)/shard_map/all_gather | solution.py:79
  15.1 141.5 %all-gather.10.cloned.1.call-start = ((), (), s32[]{:S(2)}) async-start(), calls=%async_computation.8 | async-start | bytes 5898240 | tf_op jit(solution)/shard_map/all_gather | solution.py:83
  15.8 152.3 %all-gather.12.cloned.1.call-start = ((), (), s32[]{:S(2)}) async-start(), calls=%async_computation.9 | async-start | bytes 5898240 | tf_op jit(solution)/shard_map/all_gather | solution.py:80
  16.5 82.5 %copy-start.21 = (f32[12,280]{1,0:T(8,128)}, f32[12,280]{1,0:T(8,128)S(1)}, u32[]{:S(2)}) copy-start(f32[12,280]{1,0:T(8,128)S(1)} %fusion.40) | copy-start | bytes 40324
  89.3 6.4 copy-start.4
  95.7 6.1 copy-start
  95.7 6.1 copy-start.23
  95.7 6.1 copy-start.12
  101.8 5.6 copy-start.25
  111.4 9.3 %copy-start.34 = (bf16[1,768]{1,0:T(2,128)(2,1)S(1)}, bf16[1,768]{1,0:T(2,128)(2,1)}, u32[]{:S(2)}) copy-start(bf16[1,768]{1,0:T(2,128)(2,1)} %param.26) | copy-start | bytes 4612
  111.4 39.9 %copy-start.2 = (bf16[840,768]{1,0:T(8,128)(2,1)S(1)}, bf16[840,768]{1,0:T(8,128)(2,1)}, u32[]{:S(2)}) copy-start(bf16[840,768]{1,0:T(8,128)(2,1)} %param.15) | copy-start | bytes 3870724
  111.4 39.9 %copy-start.37 = (f32[768]{0:T(1024)S(1)}, f32[768]{0:T(1024)}, u32[]{:S(2)}) copy-start(f32[768]{0:T(1024)} %param.22) | copy-start | bytes 9220
  116.9 34.4 %all-to-all-start = ((bf16[4,840,192]{1,2,0:T(8,128)(2,1)}), bf16[4,840,192]{1,2,0:T(8,128)(2,1)S(1)}, u32[]{:S(2)}, u32[]{:S(2)}) async-start(bf16[4,840,192]{1,2,0:T(8,128)(2,1)} %copy.64), calls=%async_computation | async-start | bytes 2752512 | tf_op jit(solution)/shard_map/all_to_all | solution.py:112
  120.7 234.5 %reduce-scatter.4.cloned.1.call-start = ((), (), s32[]{:S(2)}) async-start(), calls=%async_computation.12 | async-start | bytes 1474560 | tf_op jit(solution)/shard_map/reduce_scatter | solution.py:177
  156.5 11.6 %copy-start.17 = (bf16[840,768]{1,0:T(8,128)(2,1)S(1)}, bf16[840,768]{1,0:T(8,128)(2,1)}, u32[]{:S(2)}) copy-start(bf16[840,768]{1,0:T(8,128)(2,1)} %param.29) | copy-start | bytes 3870724
  168.1 31.8 %copy-start.9 = (f32[840,768]{1,0:T(8,128)S(1)}, f32[840,768]{1,0:T(8,128)}, u32[]{:S(2)}) copy-start(f32[840,768]{1,0:T(8,128)} %copy-done.8) | copy-start | bytes 7741444
  168.1 31.8 %copy-start.36 = (bf16[768,3072]{1,0:T(8,128)(2,1)S(1)}, bf16[768,3072]{1,0:T(8,128)(2,1)}, u32[]{:S(2)}) copy-start(bf16[768,3072]{1,0:T(8,128)(2,1)} %all-gather.10.cloned.1.call-done) | copy-start | bytes 14155780
  206.1 14.4 %copy-start.7 = (f32[840,768]{1,0:T(8,128)}, f32[840,768]{1,0:T(8,128)S(1)}, u32[]{:S(2)}) copy-start(f32[840,768]{1,0:T(8,128)S(1)} %get-tuple-element.39) | copy-start | bytes 7741444
  208.7 205.5 %all-gather.14.cloned.1.call-start = ((), (), s32[]{:S(2)}) async-start(), calls=%async_computation.10 | async-start | bytes 4423680 | tf_op jit(solution)/shard_map/all_gather | solution.py:164
  209.2 258.9 %reduce-scatter.6.cloned.1.call-start = ((), (), s32[]{:S(2)}) async-start(), calls=%async_computation.13 | async-start | bytes 5898240 | tf_op jit(solution)/shard_map/reduce_scatter | solution.py:185
  226.8 26.0 %all-to-all-start.1 = ((bf16[840,4,192]{0,2,1:T(8,128)(2,1)}), bf16[840,4,192]{0,2,1:T(8,128)(2,1)S(1)}, u32[]{:S(2)}, u32[]{:S(2)}) async-start(bf16[840,4,192]{0,2,1:T(8,128)(2,1)} %bitcast.6), calls=%async_computation.1 | async-start | bytes 2752512 | tf_op jit(solution)/shard_map/all_to_all | solution.py:130
  230.3 237.8 %reduce-scatter.8.cloned.1.call-start = ((), (), s32[]{:S(2)}) async-start(), calls=%async_computation.14 | async-start | bytes 5898240 | tf_op jit(solution)/shard_map/reduce_scatter | solution.py:180
  230.4 12.0 %copy-start.19 = (bf16[840,768]{1,0:T(8,128)(2,1)S(1)}, bf16[840,768]{1,0:T(8,128)(2,1)}, u32[]{:S(2)}) copy-start(bf16[840,768]{1,0:T(8,128)(2,1)} %param.29) | copy-start | bytes 3870724
  252.8 6.1 copy-start.22
  275.2 13.7 %copy-start.5 = (bf16[12,280,3,64]{1,0,3,2:T(8,128)(2,1)S(1)}, bf16[12,280,3,64]{1,0,3,2:T(8,128)(2,1)}, u32[]{:S(2)}) copy-start(bf16[12,280,3,64]{1,0,3,2:T(8,128)(2,1)} %copy-done.4) | copy-start | bytes 3870724
  331.7 5.4 copy-start.40
  331.7 77.9 %all-to-all-start.2 = ((bf16[4,840,3,192]{1,3,2,0:T(8,128)(2,1)}), bf16[4,840,3,192]{1,3,2,0:T(8,128)(2,1)}, u32[]{:S(2)}, u32[]{:S(2)}) async-start(bf16[4,840,3,192]{1,3,2,0:T(8,128)(2,1)} %pad_maximum_fusion), calls=%async_computation.2 | async-start | bytes 8257536 | tf_op jit(solution)/shard_map/all_to_all | solution.py:17
  336.8 347.4 %all-reduce.5.cloned.1.call-start = ((), (), s32[]{:S(2)}) async-start(), calls=%async_computation.11 | async-start | bytes 3538944 | tf_op jit(solution)/shard_map/psum | solution.py:188
  (23 other events, 78.2 us)
Sparse Core Ops, SparseCore 0:
  14.4 42.6 all-gather.5
  58.7 17.4 all-gather.7
  77.7 37.4 all-gather.9
  116.7 48.8 all-gather.11
  208.8 25.5 reduce-scatter.3
  235.9 32.8 all-gather.13
  271.5 47.6 reduce-scatter.5
  321.8 73.2 reduce-scatter.7
  399.6 108.7 all-reduce.4
